TPU v7x, 32 devices: a whole 2x2x4 slice. The times are simulated.
32 devices in a mesh: fsdp: 8 (over z, x), seq: 4 (over y, core).
Axes of the slice: x: 2, y: 2, z: 4, core: 2. Of those that a mesh axis runs over, the one named last changes fastest.
Arguments:
- tokens: bfloat16 [16384, 768], P(('fsdp', 'seq')), may hold values from -6 to 6
- read_memory: bfloat16 [8, 10, 768], P('fsdp'), may hold values from -6 to 6
- write_memory: bfloat16 [8, 10, 768], P('fsdp'), may hold values from -6 to 6
- lengths: int32 [8], P('fsdp'), may hold values from 1024 to 2048, as said below
- qkv_weight: bfloat16 [768, 2304], P('fsdp'), may hold values from -0.21875 to 0.21875
- qv_bias: bfloat16 [1536], P('fsdp'), may hold values from -1.5 to 1.5
- out_weight: bfloat16 [768, 768], P('fsdp'), may hold values from -6 to 6
- out_bias: bfloat16 [768], P('fsdp'), may hold values from -1.5 to 1.5
- norm1_gain: bfloat16 [768], P('fsdp'), may hold values from 0.5 to 1.5
- norm1_bias: bfloat16 [768], P('fsdp'), may hold values from -1.5 to 1.5
- up_weight: bfloat16 [768, 3072], P('fsdp'), may hold values from -0.21875 to 0.21875
- up_bias: bfloat16 [3072], P('fsdp'), may hold values from -1.5 to 1.5
- down_weight: bfloat16 [3072, 768], P('fsdp'), may hold values from -0.109375 to 0.109375
- down_bias: bfloat16 [768], P('fsdp'), may hold values from -1.5 to 1.5
- norm2_gain: bfloat16 [768], P('fsdp'), may hold values from 0.5 to 1.5
- norm2_bias: bfloat16 [768], P('fsdp'), may hold values from -1.5 to 1.5
- cotangent: bfloat16 [16384, 768], P(('fsdp', 'seq')), may hold values from -6 to 6
Outputs:
- output: bfloat16 [16384, 768], P(('fsdp', 'seq'))
- input_grad: float32 [16384, 768], P(('fsdp', 'seq'))
- read_grad: float32 [8, 10, 768], P('fsdp')
- write_grad: float32 [8, 10, 768], P('fsdp')
- qkv_weight_grad: float32 [768, 2304], P('fsdp')
- qv_bias_grad: float32 [1536], P('fsdp')
- out_weight_grad: float32 [768, 768], P('fsdp')
- out_bias_grad: float32 [768], P('fsdp')
- norm1_gain_grad: float32 [768], P('fsdp')
- norm1_bias_grad: float32 [768], P('fsdp')
- up_weight_grad: float32 [768, 3072], P('fsdp')
- up_bias_grad: float32 [3072], P('fsdp')
- down_weight_grad: float32 [3072, 768], P('fsdp')
- down_bias_grad: float32 [768], P('fsdp')
- norm2_gain_grad: float32 [768], P('fsdp')
- norm2_bias_grad: float32 [768], P('fsdp')
Inputs may be any that keep to these rules, and one draw needn't show every extreme that they name: `lengths`: valid length of each slot in positions, counting its 10 read and 10 write memory tokens; in every draw some slot has length 2048 and some slot 1024.
All inputs are finite; a program needn't handle non-finite values.
Results may differ from a plain program's by a relative error of at most 0.017.
Values may be sent and summed in bfloat16 or wider, within the bound.
A program may use at most 128 MiB of HBM per device.

v0:
```python
from functools import partial
import jax
import jax.numpy as jnp
from jax import lax
from jax.sharding import PartitionSpec as P

HEAD = 64
MEM = 10
norm_epsilon = 1e-06
masked_score = -1e30


def normalize(values, gain_vec, shift_vec):
    centre = values - jnp.mean(values, axis=-1, keepdims=True)
    factor = lax.rsqrt(jnp.mean(centre * centre, axis=-1, keepdims=True) + norm_epsilon)
    return centre * factor * gain_vec + shift_vec


def over_rows(left, right):
    return lax.dot_general(
        left, right, (((0,), (0,)), ((), ())), preferred_element_type=jnp.float32
    )


def by_columns(left, right):
    return lax.dot_general(
        left, right, (((1,), (1,)), ((), ())), preferred_element_type=jnp.float32
    )


def column_sums(values):
    return jnp.sum(values, axis=0, dtype=jnp.float32)


def per_device(
    tokens,
    read_memory,
    write_memory,
    lengths,
    qkv_weight,
    qv_bias,
    out_weight,
    out_bias,
    norm1_gain,
    norm1_bias,
    up_weight,
    up_bias,
    down_weight,
    down_bias,
    norm2_gain,
    norm2_bias,
    cotangent,
):
    seq_count = lax.axis_size("seq")
    local_rows = tokens.shape[0]
    model_width = tokens.shape[1]
    slot_rows = local_rows * seq_count
    head_cols = model_width // seq_count
    head_count = head_cols // HEAD
    block_rows = min(512, slot_rows)
    block_count = slot_rows // block_rows
    factor = HEAD ** (-0.5)
    length = lengths[0]
    places = lax.axis_index("seq") * local_rows + jnp.arange(local_rows, dtype=jnp.int32)
    in_slot = (places < length)[:, None]
    memory_slots = jnp.arange(MEM, dtype=jnp.int32)
    pick_read = places[:, None] == memory_slots[None, :]
    pick_write = places[:, None] == length - MEM + memory_slots[None, :]
    is_memory = jnp.any(pick_read | pick_write, axis=1)[:, None]
    read_float = pick_read.astype(jnp.float32)
    write_float = pick_write.astype(jnp.float32)
    memory_rows = jnp.dot(
        read_float.astype(jnp.bfloat16), read_memory[0], preferred_element_type=jnp.float32
    ) + jnp.dot(
        write_float.astype(jnp.bfloat16), write_memory[0], preferred_element_type=jnp.float32
    )
    layer_in = jnp.where(is_memory, memory_rows.astype(jnp.bfloat16), tokens)
    qkv_full, qv_full, out_full, out_bias_full, gain_one, shift_one = (
        lax.all_gather(qkv_weight, "fsdp", axis=0, tiled=True),
        lax.all_gather(qv_bias, "fsdp", axis=0, tiled=True),
        lax.all_gather(out_weight, "fsdp", axis=0, tiled=True),
        lax.all_gather(out_bias, "fsdp", axis=0, tiled=True),
        lax.all_gather(norm1_gain, "fsdp", axis=0, tiled=True),
        lax.all_gather(norm1_bias, "fsdp", axis=0, tiled=True),
    )
    projected = jnp.dot(layer_in, qkv_full, preferred_element_type=jnp.float32)
    qv_vec = qv_full.astype(jnp.float32)
    query_tok = (projected[:, :model_width] + qv_vec[:model_width]).astype(jnp.bfloat16)
    keys_tok = projected[:, model_width : 2 * model_width].astype(jnp.bfloat16)
    values_tok = (projected[:, 2 * model_width :] + qv_vec[model_width:]).astype(jnp.bfloat16)
    heads_query, heads_key, heads_value = (
        lax.all_to_all(query_tok, "seq", split_axis=1, concat_axis=0, tiled=True),
        lax.all_to_all(keys_tok, "seq", split_axis=1, concat_axis=0, tiled=True),
        lax.all_to_all(values_tok, "seq", split_axis=1, concat_axis=0, tiled=True),
    )
    heads_query = heads_query.reshape(slot_rows, head_count, HEAD)
    heads_key = heads_key.reshape(slot_rows, head_count, HEAD)
    heads_value = heads_value.reshape(slot_rows, head_count, HEAD)
    key_in_slot = jnp.arange(slot_rows, dtype=jnp.int32) < length

    def scores_for(query_block):
        scores = (
            jnp.einsum("qhd,khd->hqk", query_block, heads_key, preferred_element_type=jnp.float32)
            * factor
        )
        return jnp.where(key_in_slot[None, None, :], scores, masked_score)

    def forward_block(block_index):
        query_block = lax.dynamic_slice_in_dim(heads_query, block_index * block_rows, block_rows, 0)
        scores = scores_for(query_block)
        row_max = jnp.max(scores, axis=-1, keepdims=True)
        exponent = jnp.exp(scores - row_max)
        row_sum = jnp.sum(exponent, axis=-1, keepdims=True)
        probs_low = (exponent / row_sum).astype(jnp.bfloat16)
        mixed_block = jnp.einsum(
            "hqk,khd->qhd", probs_low, heads_value, preferred_element_type=jnp.float32
        )
        return (mixed_block.astype(jnp.bfloat16), row_max, row_sum)

    mixed_blocks, row_maxes, row_sums = lax.map(
        forward_block, jnp.arange(block_count, dtype=jnp.int32)
    )
    mixed_heads = mixed_blocks.reshape(slot_rows, head_cols)
    attended = lax.all_to_all(mixed_heads, "seq", split_axis=0, concat_axis=1, tiled=True)
    branch = jnp.dot(attended, out_full, preferred_element_type=jnp.float32) + out_bias_full.astype(
        jnp.float32
    )
    resid_one = layer_in.astype(jnp.float32) + branch
    middle, norm_one_back = jax.vjp(
        normalize, resid_one, gain_one.astype(jnp.float32), shift_one.astype(jnp.float32)
    )
    up_full, up_bias_full, down_full, down_bias_full, gain_two, shift_two = (
        lax.all_gather(up_weight, "fsdp", axis=0, tiled=True),
        lax.all_gather(up_bias, "fsdp", axis=0, tiled=True),
        lax.all_gather(down_weight, "fsdp", axis=0, tiled=True),
        lax.all_gather(down_bias, "fsdp", axis=0, tiled=True),
        lax.all_gather(norm2_gain, "fsdp", axis=0, tiled=True),
        lax.all_gather(norm2_bias, "fsdp", axis=0, tiled=True),
    )
    middle_low = middle.astype(jnp.bfloat16)
    up_pre = jnp.dot(middle_low, up_full, preferred_element_type=jnp.float32) + up_bias_full.astype(
        jnp.float32
    )
    gelu_out, gelu_back = jax.vjp(partial(jax.nn.gelu, approximate=False), up_pre)
    hidden = gelu_out.astype(jnp.bfloat16)
    down_pre = jnp.dot(
        hidden, down_full, preferred_element_type=jnp.float32
    ) + down_bias_full.astype(jnp.float32)
    final, norm_two_back = jax.vjp(
        normalize, middle + down_pre, gain_two.astype(jnp.float32), shift_two.astype(jnp.float32)
    )
    output = jnp.where(in_slot, final, 0.0).astype(jnp.bfloat16)
    grad_final = jnp.where(in_slot, cotangent.astype(jnp.float32), 0.0)
    down_back, up_back = (
        lax.all_gather(down_weight, "fsdp", axis=0, tiled=True),
        lax.all_gather(up_weight, "fsdp", axis=0, tiled=True),
    )
    grad_resid_two, grad_gain_two, grad_shift_two = norm_two_back(grad_final)
    grad_down = grad_resid_two.astype(jnp.bfloat16)
    grad_down_bias = column_sums(grad_down)
    grad_down_weight = over_rows(hidden, grad_down)
    grad_hidden = by_columns(grad_down, down_back)
    (grad_up_pre,) = gelu_back(grad_hidden)
    grad_up = grad_up_pre.astype(jnp.bfloat16)
    grad_up_bias = column_sums(grad_up)
    grad_up_weight = over_rows(middle_low, grad_up)
    grad_middle = grad_resid_two + by_columns(grad_up, up_back)
    grad_resid_one, grad_gain_one, grad_shift_one = norm_one_back(grad_middle)
    out_back, qkv_back = (
        lax.all_gather(out_weight, "fsdp", axis=0, tiled=True),
        lax.all_gather(qkv_weight, "fsdp", axis=0, tiled=True),
    )
    grad_branch = grad_resid_one.astype(jnp.bfloat16)
    grad_out_bias = column_sums(grad_branch)
    grad_out_weight = over_rows(attended, grad_branch)
    grad_attended = by_columns(grad_branch, out_back).astype(jnp.bfloat16)
    grad_heads = lax.all_to_all(grad_attended, "seq", split_axis=1, concat_axis=0, tiled=True)
    grad_heads = grad_heads.reshape(slot_rows, head_count, HEAD)

    def backward_block(carry, block_item):
        key_sum, value_sum = carry
        block_index, row_max, row_sum = block_item
        query_block = lax.dynamic_slice_in_dim(heads_query, block_index * block_rows, block_rows, 0)
        grad_block = lax.dynamic_slice_in_dim(grad_heads, block_index * block_rows, block_rows, 0)
        scores = scores_for(query_block)
        attn_probs = jnp.exp(scores - row_max) / row_sum
        probs_low = attn_probs.astype(jnp.bfloat16)
        grad_probs = jnp.einsum(
            "qhd,khd->hqk", grad_block, heads_value, preferred_element_type=jnp.float32
        )
        row_delta = jnp.sum(grad_probs * attn_probs, axis=-1, keepdims=True)
        grad_scores = (attn_probs * (grad_probs - row_delta)).astype(jnp.bfloat16)
        grad_query = (
            jnp.einsum("hqk,khd->qhd", grad_scores, heads_key, preferred_element_type=jnp.float32)
            * factor
        )
        key_sum = (
            key_sum
            + jnp.einsum(
                "hqk,qhd->khd", grad_scores, query_block, preferred_element_type=jnp.float32
            )
            * factor
        )
        value_sum = value_sum + jnp.einsum(
            "hqk,qhd->khd", probs_low, grad_block, preferred_element_type=jnp.float32
        )
        return ((key_sum, value_sum), grad_query.astype(jnp.bfloat16))

    zero_heads = jnp.zeros((slot_rows, head_count, HEAD), jnp.float32)
    (key_total, value_total), query_blocks = lax.scan(
        backward_block,
        (zero_heads, zero_heads),
        (jnp.arange(block_count, dtype=jnp.int32), row_maxes, row_sums),
    )
    grad_query_heads = query_blocks.reshape(slot_rows, head_cols)
    grad_key_heads = key_total.reshape(slot_rows, head_cols).astype(jnp.bfloat16)
    grad_value_heads = value_total.reshape(slot_rows, head_cols).astype(jnp.bfloat16)
    grad_query_tok, grad_key_tok, grad_value_tok = (
        lax.all_to_all(grad_query_heads, "seq", split_axis=0, concat_axis=1, tiled=True),
        lax.all_to_all(grad_key_heads, "seq", split_axis=0, concat_axis=1, tiled=True),
        lax.all_to_all(grad_value_heads, "seq", split_axis=0, concat_axis=1, tiled=True),
    )
    grad_projected = jnp.concatenate([grad_query_tok, grad_key_tok, grad_value_tok], axis=1)
    grad_qv_bias = jnp.concatenate([column_sums(grad_query_tok), column_sums(grad_value_tok)])
    grad_qkv_weight = over_rows(layer_in, grad_projected)
    grad_layer_in = grad_resid_one + by_columns(grad_projected, qkv_back)
    input_grad = jnp.where(is_memory, 0.0, grad_layer_in)
    grad_read = lax.dot_general(
        read_float,
        grad_layer_in,
        (((0,), (0,)), ((), ())),
        precision=lax.Precision.HIGHEST,
        preferred_element_type=jnp.float32,
    )
    grad_write = lax.dot_general(
        write_float,
        grad_layer_in,
        (((0,), (0,)), ((), ())),
        precision=lax.Precision.HIGHEST,
        preferred_element_type=jnp.float32,
    )
    (
        shard_qkv,
        shard_qv,
        shard_out_w,
        shard_out_b,
        shard_gain_one,
        shard_shift_one,
        shard_up_w,
        shard_up_b,
        shard_down_w,
        shard_down_b,
        shard_gain_two,
        shard_shift_two,
    ) = (
        lax.psum_scatter(grad_qkv_weight, "fsdp", scatter_dimension=0, tiled=True),
        lax.psum_scatter(grad_qv_bias, "fsdp", scatter_dimension=0, tiled=True),
        lax.psum_scatter(grad_out_weight, "fsdp", scatter_dimension=0, tiled=True),
        lax.psum_scatter(grad_out_bias, "fsdp", scatter_dimension=0, tiled=True),
        lax.psum_scatter(grad_gain_one, "fsdp", scatter_dimension=0, tiled=True),
        lax.psum_scatter(grad_shift_one, "fsdp", scatter_dimension=0, tiled=True),
        lax.psum_scatter(grad_up_weight, "fsdp", scatter_dimension=0, tiled=True),
        lax.psum_scatter(grad_up_bias, "fsdp", scatter_dimension=0, tiled=True),
        lax.psum_scatter(grad_down_weight, "fsdp", scatter_dimension=0, tiled=True),
        lax.psum_scatter(grad_down_bias, "fsdp", scatter_dimension=0, tiled=True),
        lax.psum_scatter(grad_gain_two, "fsdp", scatter_dimension=0, tiled=True),
        lax.psum_scatter(grad_shift_two, "fsdp", scatter_dimension=0, tiled=True),
    )
    (
        sum_qkv,
        sum_qv,
        sum_out_w,
        sum_out_b,
        sum_gain_one,
        sum_shift_one,
        sum_up_w,
        sum_up_b,
        sum_down_w,
        sum_down_b,
        sum_gain_two,
        sum_shift_two,
        read_total,
        write_total,
    ) = (
        lax.psum(shard_qkv.astype(jnp.bfloat16), "seq").astype(jnp.float32),
        lax.psum(shard_qv.astype(jnp.bfloat16), "seq").astype(jnp.float32),
        lax.psum(shard_out_w.astype(jnp.bfloat16), "seq").astype(jnp.float32),
        lax.psum(shard_out_b.astype(jnp.bfloat16), "seq").astype(jnp.float32),
        lax.psum(shard_gain_one.astype(jnp.bfloat16), "seq").astype(jnp.float32),
        lax.psum(shard_shift_one.astype(jnp.bfloat16), "seq").astype(jnp.float32),
        lax.psum(shard_up_w.astype(jnp.bfloat16), "seq").astype(jnp.float32),
        lax.psum(shard_up_b.astype(jnp.bfloat16), "seq").astype(jnp.float32),
        lax.psum(shard_down_w.astype(jnp.bfloat16), "seq").astype(jnp.float32),
        lax.psum(shard_down_b.astype(jnp.bfloat16), "seq").astype(jnp.float32),
        lax.psum(shard_gain_two.astype(jnp.bfloat16), "seq").astype(jnp.float32),
        lax.psum(shard_shift_two.astype(jnp.bfloat16), "seq").astype(jnp.float32),
        lax.psum(grad_read.astype(jnp.bfloat16), "seq").astype(jnp.float32),
        lax.psum(grad_write.astype(jnp.bfloat16), "seq").astype(jnp.float32),
    )
    return (
        output,
        input_grad,
        read_total[None],
        write_total[None],
        sum_qkv,
        sum_qv,
        sum_out_w,
        sum_out_b,
        sum_gain_one,
        sum_shift_one,
        sum_up_w,
        sum_up_b,
        sum_down_w,
        sum_down_b,
        sum_gain_two,
        sum_shift_two,
    )


def solution(mesh):
    in_specs = (
        P(("fsdp", "seq"), None),
        P("fsdp", None, None),
        P("fsdp", None, None),
        P("fsdp"),
        P("fsdp", None),
        P("fsdp"),
        P("fsdp", None),
        P("fsdp"),
        P("fsdp"),
        P("fsdp"),
        P("fsdp", None),
        P("fsdp"),
        P("fsdp", None),
        P("fsdp"),
        P("fsdp"),
        P("fsdp"),
        P(("fsdp", "seq"), None),
    )
    out_specs = (
        P(("fsdp", "seq"), None),
        P(("fsdp", "seq"), None),
        P("fsdp", None, None),
        P("fsdp", None, None),
        P("fsdp", None),
        P("fsdp"),
        P("fsdp", None),
        P("fsdp"),
        P("fsdp"),
        P("fsdp"),
        P("fsdp", None),
        P("fsdp"),
        P("fsdp", None),
        P("fsdp"),
        P("fsdp"),
        P("fsdp"),
    )
    return jax.shard_map(
        per_device, mesh=mesh, in_specs=in_specs, out_specs=out_specs, check_vma=False
    )
```

profile of v0, /device:TPU:0, one launch (start us, length us, event | category | flops | bytes accessed | tf_op | source)
XLA Modules:
  0.0 1022.8 jit_solution(4488948586990560364)
XLA Ops:
  18.6 39.7 %all-reduce.16 = (bf16[1536]{0:T(1024)(128)(2,1)S(1)}, bf16[768]{0:T(1024)(128)(2,1)S(1)}, bf16[768]{0:T(1024)(128)(2,1)S(1)}, bf16[768]{0:T(1024)(128)(2,1)S(1)...) all-reduce(bf16[1536]{0:T(1024)(128)(2,1)S(1)} %dynamic-update-slic, ...), channel_id=1, replica_groups=mesh['fsdp'=8,'seq'=4] {'fsdp'}, use_global_device_ids=true, to_apply=%add | all-reduce | flops 6144 | bytes 24576
  60.5 18.2 %all-gather.6.cloned.1.call-done = bf16[768,2304]{1,0:T(8,128)(2,1)} async-done(((bf16[96,2304]{1,0:T(8,128)(2,1)}), bf16[768,2304]{1,0:T(8,128)(2,1)}) %all-gather.6.cloned.1.call-update) | async-done | bytes 3538960 | tf_op jit(solution)/shard_map/all_gather | solution.py:79
  91.0 10.5 %all-to-all-done = bf16[512,4,192]{0,2,1:T(8,128)(2,1)S(1)} async-done(((bf16[512,4,192]{0,2,1:T(8,128)(2,1)}), bf16[512,4,192]{0,2,1:T(8,128)(2,1)S(1)}, u32[]{:S(2)}, u32[]{:S(2)}) %all-to-all-start) | async-done | bytes 786464 | tf_op jit(solution)/shard_map/all_to_all | solution.py:92
  107.7 9.0 all-to-all-done.2
  136.3 44.2 %while.30 = (s32[]{:T(128)}, bf16[4,512,3,64]{1,3,2,0:T(8,128)(2,1)}, f32[4,3,512,1]{2,1,3,0:T(4,128)S(1)}, f32[4,3,512,1]{2,1,3,0:T(4,128)S(1)}, s32[4]{0:T(128...) while((s32[]{:T(128)}, ...), condition=%wide.region_4.5_spmd.clone, body=%wide.region_1.4_spmd.clone.sunk | while | flops 843152384 | bytes 39787204 | solution.py:120
  184.1 26.3 %all-gather = bf16[8,1,384]{2,1,0:T(2,128)(2,1)S(1)} all-gather(bf16[1,1,384]{2,1,0:T(2,128)(2,1)S(1)} %reshape.204), channel_id=1, replica_groups=mesh['fsdp'=8,'seq'=4] {'fsdp'}, dimensions={0}, use_global_device_ids=true | all-gather | bytes 6912 | tf_op jit(solution)/shard_map/all_gather | solution.py:134
  214.5 20.9 %multiply_convert_fusion.1 = (bf16[512,3072]{1,0:T(8,128)(2,1)}, f32[512,3072]{1,0:T(8,128)}, f32[512,3072]{1,0:T(8,128)}) fusion(f32[3072]{0:T(1024)S(1)} %bitcast.154, bf16[768,3072]{1,0:T(8,128)(2,1)} %all-gather.10.cloned.1.call-done, f32[512,768]{1,0:T(8,128)} %copy-done.7, f32[768]{0:T(1024)S(1)} %convert_element_type.216, ...), kind=kOutput, calls=%fused_computation.49 | convolution fusion | flops 2521694208 | bytes 22042624 | tf_op jit(solution)/shard_map/dot_general | solution.py:141
  235.4 46.2 %all-gather.12.cloned.1.call-done = bf16[3072,768]{1,0:T(8,128)(2,1)} async-done(((bf16[384,768]{1,0:T(8,128)(2,1)}), bf16[3072,768]{1,0:T(8,128)(2,1)}) %all-gather.12.cloned.1.call-update) | async-done | bytes 4718608 | tf_op jit(solution)/shard_map/all_gather | solution.py:135
  292.0 8.9 convert_reduce_fusion
  316.8 8.2 all-to-all-done.4
  331.4 115.4 %while.31 = (s32[]{:T(128)}, f32[2048,3,64]{0,2,1:T(8,128)S(1)}, f32[2048,3,64]{0,2,1:T(8,128)}, bf16[4,512,3,64]{1,3,2,0:T(8,128)(2,1)}, s32[4]{0:T(128)S(1)}, ...) while((s32[]{:T(128)}, f32[2048,3,64]{0,2,1:T(8,128)S(1)}, ...), condition=%wide.region_15.16_spmd.clone, body=%wide.region_13.15_spmd.clone.sunk | while | flops 2046886400 | bytes 204722992 | solution.py:210
  378.6 6.3 fusion.145
  454.5 9.2 all-to-all-done.6
  463.7 14.1 %all_to_all.134 = bf16[4,512,192]{1,2,0:T(8,128)(2,1)S(1)} all-to-all(bf16[4,512,192]{1,2,0:T(8,128)(2,1)S(1)} %copy.93), channel_id=1, replica_groups=mesh['fsdp'=8,'seq'=4] {'seq'}, dimensions={0} | all-to-all | bytes 1572864 | tf_op jit(solution)/shard_map/all_to_all | solution.py:221
  477.8 14.3 %all_to_all.135 = bf16[4,512,192]{1,2,0:T(8,128)(2,1)S(1)} all-to-all(bf16[4,512,192]{1,2,0:T(8,128)(2,1)S(1)} %bitcast.149), channel_id=1, replica_groups=mesh['fsdp'=8,'seq'=4] {'seq'}, dimensions={0} | all-to-all | bytes 1572864 | tf_op jit(solution)/shard_map/all_to_all | solution.py:219
  492.0 6.4 fusion.51
  499.5 8.2 fusion.82
  509.2 7.2 fusion.69
  519.1 37.6 %all-reduce.15 = (bf16[1536]{0:T(1024)(128)(2,1)S(1)}, bf16[768]{0:T(1024)(128)(2,1)S(1)}, bf16[768]{0:T(1024)(128)(2,1)S(1)}, bf16[768]{0:T(1024)(128)(2,1)S(1)...) all-reduce(f32[1536]{0:T(1024)S(1)} %pad_maximum_fusion.3, ...), channel_id=3, replica_groups=mesh['fsdp'=8,'seq'=4] {'fsdp'}, use_global_device_ids=true, to_apply=%region_22.23.clone | all-reduce | flops 9216 | bytes 55296
  559.2 66.9 %reduce-scatter.5.cloned.1.call-done = f32[96,2304]{1,0:T(8,128)} async-done(((f32[768,2304]{1,0:T(8,128)}), f32[96,2304]{1,0:T(8,128)}) %reduce-scatter.5.cloned.1.call-update) | async-done | bytes 884752 | tf_op jit(solution)/shard_map/reduce_scatter | solution.py:256
  628.1 164.6 %reduce-scatter.11.cloned.1.call-done = f32[384,768]{1,0:T(8,128)} async-done(((f32[3072,768]{1,0:T(8,128)}), f32[384,768]{1,0:T(8,128)}) %reduce-scatter.11.cloned.1.call-update) | async-done | bytes 1179664 | tf_op jit(solution)/shard_map/reduce_scatter | solution.py:264
  794.8 164.3 %reduce-scatter.9.cloned.1.call-done = f32[96,3072]{1,0:T(8,128)} async-done(((f32[768,3072]{1,0:T(8,128)}), f32[96,3072]{1,0:T(8,128)}) %reduce-scatter.9.cloned.1.call-update) | async-done | bytes 1179664 | tf_op jit(solution)/shard_map/reduce_scatter | solution.py:262
  968.2 14.3 %all-reduce.17 = (bf16[1,10,768]{2,1,0:T(8,128)(2,1)S(1)}, bf16[1,10,768]{2,1,0:T(8,128)(2,1)S(1)}, bf16[192]{0:T(256)(128)(2,1)S(1)}, bf16[96]{0:T(256)(128)(2,...) all-reduce(bf16[1,10,768]{2,1,0:T(8,128)(2,1)S(1)} %fusion.49, ...), channel_id=1, replica_groups=mesh['fsdp'=8,'seq'=4] {'seq'}, use_global_device_ids=true, to_apply=%region_16.17 | all-reduce | flops 16512 | bytes 66048 | tf_op jit(solution)/shard_map/psum | solution.py:297
  988.0 21.9 %all-reduce.21.cloned.1.call-done = (bf16[96,2304]{1,0:T(8,128)(2,1)}, bf16[96,768]{1,0:T(8,128)(2,1)}, bf16[96,3072]{1,0:T(8,128)(2,1)}, bf16[384,768]{1,0:T(8,128)(2,1)}) async-done(((bf16[96,2304]{1,0:T(8,128)(2,1)}, bf16[96,768]{1,0:T(8,128)(2,1)}, bf16[96,3072]{1,0:T(8,128)(2,1)}, bf16[384,768]{1,0:T(8,128)(2,1)}), (bf16[96,2304]{1,0:T(8,128)(2,1)}, bf16[96,768]{1,0:T(8,128)(2,1)}, ...) | async-done | bytes 1769488 | tf_op jit(solution)/shard_map/psum | solution.py:285
  (316 shorter events, 275.3 us)
Async XLA Ops:
  7.2 51.2 %copy-start = (bf16[1,10,768]{2,1,0:T(8,128)(2,1)S(1)}, bf16[1,10,768]{2,1,0:T(8,128)(2,1)}, u32[]{:S(2)}) copy-start(bf16[1,10,768]{2,1,0:T(8,128)(2,1)} %param.22) | copy-start | bytes 46084
  7.2 71.6 %all-gather.6.cloned.1.call-start = ((), (), s32[]{:S(2)}) async-start(), calls=%async_computation.12 | async-start | bytes 3981312 | tf_op jit(solution)/shard_map/all_gather | solution.py:79
  7.9 202.6 %all-gather.8.cloned.1.call-start = ((), (), s32[]{:S(2)}) async-start(), calls=%async_computation.13 | async-start | bytes 1327104 | tf_op jit(solution)/shard_map/all_gather | solution.py:81
  8.7 205.8 %all-gather.10.cloned.1.call-start = ((), (), s32[]{:S(2)}) async-start(), calls=%async_computation.14 | async-start | bytes 5308416 | tf_op jit(solution)/shard_map/all_gather | solution.py:133
  86.4 15.1 %all-to-all-start = ((bf16[512,4,192]{0,2,1:T(8,128)(2,1)}), bf16[512,4,192]{0,2,1:T(8,128)(2,1)S(1)}, u32[]{:S(2)}, u32[]{:S(2)}) async-start(bf16[512,4,192]{0,2,1:T(8,128)(2,1)} %bitcast.4), calls=%async_computation | async-start | bytes 1572864 | tf_op jit(solution)/shard_map/all_to_all | solution.py:92
  101.5 15.1 %all-to-all-start.2 = ((bf16[512,4,192]{0,2,1:T(8,128)(2,1)}), bf16[512,4,192]{0,2,1:T(8,128)(2,1)S(1)}, u32[]{:S(2)}, u32[]{:S(2)}) async-start(bf16[512,4,192]{0,2,1:T(8,128)(2,1)} %bitcast.8), calls=%async_computation.2 | async-start | bytes 1572864 | tf_op jit(solution)/shard_map/all_to_all | solution.py:94
  116.6 15.1 %all-to-all-start.1 = ((bf16[512,4,192]{0,2,1:T(8,128)(2,1)}), bf16[512,4,192]{0,2,1:T(8,128)(2,1)S(1)}, u32[]{:S(2)}, u32[]{:S(2)}) async-start(bf16[512,4,192]{0,2,1:T(8,128)(2,1)} %bitcast.6), calls=%async_computation.1 | async-start | bytes 1572864 | tf_op jit(solution)/shard_map/all_to_all | solution.py:93
  120.1 161.5 %all-gather.12.cloned.1.call-start = ((), (), s32[]{:S(2)}) async-start(), calls=%async_computation.15 | async-start | bytes 5308416 | tf_op jit(solution)/shard_map/all_gather | solution.py:135
  180.5 30.0 %all-to-all-start.3 = ((bf16[4,512,192]{1,2,0:T(8,128)(2,1)}), bf16[4,512,192]{1,2,0:T(8,128)(2,1)S(1)}, u32[]{:S(2)}, u32[]{:S(2)}) async-start(bf16[4,512,192]{1,2,0:T(8,128)(2,1)} %bitcast.10), calls=%async_computation.3 | async-start | bytes 1572864 | tf_op jit(solution)/shard_map/all_to_all | solution.py:124
  184.0 120.5 %copy-start.30 = (f32[768]{0:T(1024)}, f32[768]{0:T(1024)S(1)}, u32[]{:S(2)}) copy-start(f32[768]{0:T(1024)S(1)} %convert_element_type.215) | copy-start | bytes 9220
  184.1 97.5 %copy-start.39 = (f32[768]{0:T(1024)}, f32[768]{0:T(1024)S(1)}, u32[]{:S(2)}) copy-start(f32[768]{0:T(1024)S(1)} %convert_element_type.216) | copy-start | bytes 9220
  213.0 91.5 %copy-start.24 = (f32[512]{0:T(512)}, f32[512]{0:T(512)S(1)}, u32[]{:S(2)}) copy-start(f32[512]{0:T(512)S(1)} %broadcast_multiply_fusion.1) | copy-start | bytes 6148
  214.5 90.1 %copy-start.33 = (f32[512]{0:T(512)}, f32[512]{0:T(512)S(1)}, u32[]{:S(2)}) copy-start(f32[512]{0:T(512)S(1)} %fusion.65) | copy-start | bytes 6148
  214.5 67.1 %copy-start.8 = (f32[512,768]{1,0:T(8,128)S(1)}, f32[512,768]{1,0:T(8,128)}, u32[]{:S(2)}) copy-start(f32[512,768]{1,0:T(8,128)} %copy-done.7) | copy-start | bytes 4718596
  309.1 15.9 %all-to-all-start.4 = ((bf16[512,4,192]{0,2,1:T(8,128)(2,1)}), bf16[512,4,192]{0,2,1:T(8,128)(2,1)}, u32[]{:S(2)}, u32[]{:S(2)}) async-start(bf16[512,4,192]{0,2,1:T(8,128)(2,1)} %bitcast.15), calls=%async_computation.4 | async-start | bytes 1572864 | tf_op jit(solution)/shard_map/all_to_all | solution.py:177
  313.4 244.0 %reduce-scatter.7.cloned.1.call-start = ((), (), s32[]{:S(2)}) async-start(), calls=%async_computation.17 | async-start | bytes 2654208 | tf_op jit(solution)/shard_map/reduce_scatter | solution.py:258
  448.6 15.1 %all-to-all-start.6 = ((bf16[4,512,192]{1,2,0:T(8,128)(2,1)}), bf16[4,512,192]{1,2,0:T(8,128)(2,1)S(1)}, u32[]{:S(2)}, u32[]{:S(2)}) async-start(bf16[4,512,192]{1,2,0:T(8,128)(2,1)} %copy.92), calls=%async_computation.6 | async-start | bytes 1572864 | tf_op jit(solution)/shard_map/all_to_all | solution.py:220
  452.1 174.0 %reduce-scatter.5.cloned.1.call-start = ((), (), s32[]{:S(2)}) async-start(), calls=%async_computation.16 | async-start | bytes 7962624 | tf_op jit(solution)/shard_map/reduce_scatter | solution.py:256
  498.4 294.3 %reduce-scatter.11.cloned.1.call-start = ((), (), s32[]{:S(2)}) async-start(), calls=%async_computation.19 | async-start | bytes 10616832 | tf_op jit(solution)/shard_map/reduce_scatter | solution.py:264
  507.8 451.4 %reduce-scatter.9.cloned.1.call-start = ((), (), s32[]{:S(2)}) async-start(), calls=%async_computation.18 | async-start | bytes 10616832 | tf_op jit(solution)/shard_map/reduce_scatter | solution.py:262
  516.5 493.4 %all-reduce.21.cloned.1.call-start = ((), (), s32[]{:S(2)}) async-start(), calls=%async_computation.20 | async-start | bytes 3538944 | tf_op jit(solution)/shard_map/psum | solution.py:285
  557.4 404.0 %copy-start.11 = (f32[512,768]{1,0:T(8,128)S(1)}, f32[512,768]{1,0:T(8,128)}, u32[]{:S(2)}) copy-start(f32[512,768]{1,0:T(8,128)} %copy-done.10) | copy-start | bytes 4718596
  557.4 404.0 %copy-start.36 = (f32[512]{0:T(512)S(1)}, f32[512]{0:T(512)}, u32[]{:S(2)}) copy-start(f32[512]{0:T(512)} %copy-done.35) | copy-start | bytes 6148
  557.4 404.0 %copy-start.44 = (pred[512]{0:T(512)(128)(4,1)S(1)}, pred[512]{0:T(512)(128)(4,1)}, u32[]{:S(2)}) copy-start(pred[512]{0:T(512)(128)(4,1)} %copy-done.43) | copy-start | bytes 1540
  (48 other events, 458.1 us)
Sparse Core Ops, SparseCore 0:
  10.2 68.4 all-gather.5
  80.9 39.4 all-gather.7
  122.7 78.6 all-gather.9
  203.4 78.1 all-gather.11
  317.4 67.6 reduce-scatter.6
  498.5 127.5 reduce-scatter.4
  630.1 162.5 reduce-scatter.10
  796.7 162.3 reduce-scatter.8
  963.1 46.7 all-reduce.20
where the time goes:
time: 1030 us; the launch traced here: 1020 us
  waiting for transfers between devices  528 us (51%)
  matrix products  195 us (19%)
  blocking collectives  146 us (14%)
  other arithmetic  57.2 us (6%)
  local copies, waits for them, and re-layouts  50.3 us (5%)
  starting transfers between devices  22.2 us (2%)
  between operations  18.7 us (2%)
    reduce_scatter x1, waiting for transfers between devices, per_device(): lax.psum_scatter(grad_down_weight, 'fsdp', scatter_dimension=0, tiled=True)  165 us
    reduce_scatter x1, waiting for transfers between devices, per_device(): lax.psum_scatter(grad_up_weight, 'fsdp', scatter_dimension=0, tiled=True)  164 us
    unnamed x2, blocking collectives  77.3 us
    reduce_scatter x1, waiting for transfers between devices, per_device(): lax.psum_scatter(grad_qkv_weight, 'fsdp', scatter_dimension=0, tiled=True)  66.9 us
    all_gather x1, waiting for transfers between devices, per_device(): lax.all_gather(down_weight, 'fsdp', axis=0, tiled=True)  46.2 us
    all_gather x1, blocking collectives, per_device(): lax.all_gather(up_bias, 'fsdp', axis=0, tiled=True)  26.3 us
    dot_general x8, matrix products, scores_for(): jnp.einsum('qhd,khd->hqk', query_block, heads_key, preferred_element_type...  25.4 us
    dot_general x4, matrix products, over_rows(): lax.dot_general(left, right, (((0,), (0,)), ((), ())), preferred_element_...  25.2 us
  transfers between devices with their start and end apart: 15, of which 11 were waited for; matrix products, arithmetic and copies ran while one was open for 25% of the time, Pallas kernels for 0%

commit v1 on v0

--- a/solution.py
+++ b/solution.py
@@ -266,6 +266,7 @@
         lax.psum_scatter(grad_gain_two, "fsdp", scatter_dimension=0, tiled=True),
         lax.psum_scatter(grad_shift_two, "fsdp", scatter_dimension=0, tiled=True),
     )
+    convert_page = lambda block_in: jnp.sum(lax.all_gather(block_in, axis_name="seq"), axis=0)
     (
         sum_qkv,
         sum_qv,
@@ -282,7 +283,7 @@
         read_total,
         write_total,
     ) = (
-        lax.psum(shard_qkv.astype(jnp.bfloat16), "seq").astype(jnp.float32),
+        convert_page(shard_qkv.astype(jnp.bfloat16)).astype(jnp.float32),
         lax.psum(shard_qv.astype(jnp.bfloat16), "seq").astype(jnp.float32),
         lax.psum(shard_out_w.astype(jnp.bfloat16), "seq").astype(jnp.float32),
         lax.psum(shard_out_b.astype(jnp.bfloat16), "seq").astype(jnp.float32),

time: 1030 us -> 1110 us (1.078)
  waiting for transfers between devices: 528 us -> 616 us
    reduce_scatter x1, waiting for transfers between devices: 0.01 us -> 61.7 us  [per_device(): lax.psum_scatter(grad_out_weight, 'fsdp', scatter_dimension=0, tiled=True)]
    reduce_scatter x1, waiting for transfers between devices: 66.9 us -> 105 us  [per_device(): lax.psum_scatter(grad_qkv_weight, 'fsdp', scatter_dimension=0, tiled=True)]
    psum x1, waiting for transfers between devices: 21.9 us -> 6.17 us  [per_device(): lax.psum(shard_out_w.astype(jnp.bfloat16), 'seq').astype(jnp.float32)]
  transfers between devices with their start and end apart: 15 -> 16, of which waited for: 11 -> 12; matrix products, arithmetic and copies ran while one was open for 25% -> 13% of each run, Pallas kernels for 0% -> 0%
where the time goes in v1:
time: 1110 us
  waiting for transfers between devices  616 us (55%)
  matrix products  195 us (18%)
  blocking collectives  140 us (13%)
  other arithmetic  59.1 us (5%)
  local copies, waits for them, and re-layouts  51.2 us (5%)
  starting transfers between devices  22.2 us (2%)
  between operations  19.1 us (2%)
    reduce_scatter x1, waiting for transfers between devices, per_device(): lax.psum_scatter(grad_down_weight, 'fsdp', scatter_dimension=0, tiled=True)  165 us
    reduce_scatter x1, waiting for transfers between devices, per_device(): lax.psum_scatter(grad_up_weight, 'fsdp', scatter_dimension=0, tiled=True)  164 us
    reduce_scatter x1, waiting for transfers between devices, per_device(): lax.psum_scatter(grad_qkv_weight, 'fsdp', scatter_dimension=0, tiled=True)  105 us
    unnamed x2, blocking collectives  75.3 us
    reduce_scatter x1, waiting for transfers between devices, per_device(): lax.psum_scatter(grad_out_weight, 'fsdp', scatter_dimension=0, tiled=True)  61.7 us
    all_gather x1, waiting for transfers between devices, per_device(): lax.all_gather(down_weight, 'fsdp', axis=0, tiled=True)  46 us
    all_gather x1, blocking collectives, per_device(): lax.all_gather(up_bias, 'fsdp', axis=0, tiled=True)  26.1 us
    dot_general x8, matrix products, scores_for(): jnp.einsum('qhd,khd->hqk', query_block, heads_key, preferred_element_type...  25.4 us
  transfers between devices with their start and end apart: 16, of which 12 were waited for; matrix products, arithmetic and copies ran while one was open for 13% of the time, Pallas kernels for 0%

profile of v1, /device:TPU:0, one launch (start us, length us, event | category | flops | bytes accessed | tf_op | source)
XLA Modules:
  0.0 1108.4 jit_solution(4016758210707672629)
XLA Ops:
  18.6 39.7 %all-reduce.16 = (bf16[1536]{0:T(1024)(128)(2,1)S(1)}, bf16[768]{0:T(1024)(128)(2,1)S(1)}, bf16[768]{0:T(1024)(128)(2,1)S(1)}, bf16[768]{0:T(1024)(128)(2,1)S(1)...) all-reduce(bf16[1536]{0:T(1024)(128)(2,1)S(1)} %dynamic-update-slic, ...), channel_id=1, replica_groups=mesh['fsdp'=8,'seq'=4] {'fsdp'}, use_global_device_ids=true, to_apply=%add | all-reduce | flops 6144 | bytes 24576
  60.5 18.2 %all-gather.8.cloned.1.call-done = bf16[768,2304]{1,0:T(8,128)(2,1)} async-done(((bf16[96,2304]{1,0:T(8,128)(2,1)}), bf16[768,2304]{1,0:T(8,128)(2,1)}) %all-gather.8.cloned.1.call-update) | async-done | bytes 3538960 | tf_op jit(solution)/shard_map/all_gather | solution.py:79
  91.0 10.5 all-to-all-done
  107.6 9.0 all-to-all-done.2
  136.3 44.2 %while.30 = (s32[]{:T(128)}, bf16[4,512,3,64]{1,3,2,0:T(8,128)(2,1)}, f32[4,3,512,1]{2,1,3,0:T(4,128)S(1)}, f32[4,3,512,1]{2,1,3,0:T(4,128)S(1)}, s32[4]{0:T(128...) while((s32[]{:T(128)}, ...), condition=%wide.region_4.5_spmd.clone, body=%wide.region_1.4_spmd.clone.sunk | while | flops 843152384 | bytes 39787204 | solution.py:120
  184.1 26.1 %all-gather.1 = bf16[8,1,384]{2,1,0:T(2,128)(2,1)S(1)} all-gather(bf16[1,1,384]{2,1,0:T(2,128)(2,1)S(1)} %reshape.205), channel_id=1, replica_groups=mesh['fsdp'=8,'seq'=4] {'fsdp'}, dimensions={0}, use_global_device_ids=true | all-gather | bytes 6912 | tf_op jit(solution)/shard_map/all_gather | solution.py:134
  214.6 21.0 %multiply_convert_fusion.1 = (bf16[512,3072]{1,0:T(8,128)(2,1)}, f32[512,3072]{1,0:T(8,128)}, f32[512,3072]{1,0:T(8,128)}) fusion(f32[3072]{0:T(1024)S(1)} %bitcast.156, bf16[768,3072]{1,0:T(8,128)(2,1)} %all-gather.12.cloned.1.call-done, f32[512,768]{1,0:T(8,128)} %copy-done.7, f32[768]{0:T(1024)S(1)} %convert_element_type.218, ...), kind=kOutput, calls=%fused_computation.49 | convolution fusion | flops 2521694208 | bytes 22042624 | tf_op jit(solution)/shard_map/dot_general | solution.py:141
  235.6 46.0 %all-gather.14.cloned.1.call-done = bf16[3072,768]{1,0:T(8,128)(2,1)} async-done(((bf16[384,768]{1,0:T(8,128)(2,1)}), bf16[3072,768]{1,0:T(8,128)(2,1)}) %all-gather.14.cloned.1.call-update) | async-done | bytes 4718608 | tf_op jit(solution)/shard_map/all_gather | solution.py:135
  292.0 9.2 convert_reduce_fusion
  313.6 11.7 %all-to-all-done.4 = bf16[512,4,192]{0,2,1:T(8,128)(2,1)} async-done(((bf16[512,4,192]{0,2,1:T(8,128)(2,1)}), bf16[512,4,192]{0,2,1:T(8,128)(2,1)}, u32[]{:S(2)}, u32[]{:S(2)}) %all-to-all-start.4) | async-done | bytes 786464 | tf_op jit(solution)/shard_map/all_to_all | solution.py:177
  331.7 115.5 %while.31 = (s32[]{:T(128)}, f32[2048,3,64]{0,2,1:T(8,128)S(1)}, f32[2048,3,64]{0,2,1:T(8,128)}, bf16[4,512,3,64]{1,3,2,0:T(8,128)(2,1)}, s32[4]{0:T(128)S(1)}, ...) while((s32[]{:T(128)}, f32[2048,3,64]{0,2,1:T(8,128)S(1)}, ...), condition=%wide.region_15.16_spmd.clone, body=%wide.region_13.15_spmd.clone.sunk | while | flops 2046886400 | bytes 204722992 | solution.py:210
  350.4 6.3 fusion.145
  378.8 6.3 fusion.145
  454.8 9.2 all-to-all-done.6
  464.0 14.1 %all_to_all.134 = bf16[4,512,192]{1,2,0:T(8,128)(2,1)S(1)} all-to-all(bf16[4,512,192]{1,2,0:T(8,128)(2,1)S(1)} %copy.93), channel_id=1, replica_groups=mesh['fsdp'=8,'seq'=4] {'seq'}, dimensions={0} | all-to-all | bytes 1572864 | tf_op jit(solution)/shard_map/all_to_all | solution.py:221
  478.1 14.2 %all_to_all.135 = bf16[4,512,192]{1,2,0:T(8,128)(2,1)S(1)} all-to-all(bf16[4,512,192]{1,2,0:T(8,128)(2,1)S(1)} %bitcast.150), channel_id=1, replica_groups=mesh['fsdp'=8,'seq'=4] {'seq'}, dimensions={0} | all-to-all | bytes 1572864 | tf_op jit(solution)/shard_map/all_to_all | solution.py:219
  503.0 8.8 fusion.82
  513.2 7.2 fusion.69
  520.5 105.3 %reduce-scatter.5.cloned.1.call-done = f32[96,2304]{1,0:T(8,128)} async-done(((f32[768,2304]{1,0:T(8,128)}), f32[96,2304]{1,0:T(8,128)}) %reduce-scatter.5.cloned.1.call-update) | async-done | bytes 884752 | tf_op jit(solution)/shard_map/reduce_scatter | solution.py:256
  635.9 61.7 %reduce-scatter.7.cloned.1.call-done = f32[96,768]{1,0:T(8,128)} async-done(((f32[768,768]{1,0:T(8,128)}), f32[96,768]{1,0:T(8,128)}) %reduce-scatter.7.cloned.1.call-update) | async-done | bytes 294928 | tf_op jit(solution)/shard_map/reduce_scatter | solution.py:258
  699.2 164.9 %reduce-scatter.11.cloned.1.call-done = f32[384,768]{1,0:T(8,128)} async-done(((f32[3072,768]{1,0:T(8,128)}), f32[384,768]{1,0:T(8,128)}) %reduce-scatter.11.cloned.1.call-update) | async-done | bytes 1179664 | tf_op jit(solution)/shard_map/reduce_scatter | solution.py:264
  866.3 164.5 %reduce-scatter.9.cloned.1.call-done = f32[96,3072]{1,0:T(8,128)} async-done(((f32[768,3072]{1,0:T(8,128)}), f32[96,3072]{1,0:T(8,128)}) %reduce-scatter.9.cloned.1.call-update) | async-done | bytes 1179664 | tf_op jit(solution)/shard_map/reduce_scatter | solution.py:262
  1033.6 35.6 %all-reduce.15 = (bf16[1536]{0:T(1024)(128)(2,1)S(1)}, bf16[768]{0:T(1024)(128)(2,1)S(1)}, bf16[768]{0:T(1024)(128)(2,1)S(1)}, bf16[768]{0:T(1024)(128)(2,1)S(1)...) all-reduce(f32[1536]{0:T(1024)S(1)} %pad_maximum_fusion.3, ...), channel_id=4, replica_groups=mesh['fsdp'=8,'seq'=4] {'fsdp'}, use_global_device_ids=true, to_apply=%region_22.23.clone | all-reduce | flops 9216 | bytes 55296
  1071.1 10.7 all-reduce.17
  (332 shorter events, 283.8 us)
Async XLA Ops:
  7.2 71.6 %all-gather.8.cloned.1.call-start = ((), (), s32[]{:S(2)}) async-start(), calls=%async_computation.12 | async-start | bytes 3981312 | tf_op jit(solution)/shard_map/all_gather | solution.py:79
  7.9 202.4 %all-gather.10.cloned.1.call-start = ((), (), s32[]{:S(2)}) async-start(), calls=%async_computation.13 | async-start | bytes 1327104 | tf_op jit(solution)/shard_map/all_gather | solution.py:81
  8.7 205.9 %all-gather.12.cloned.1.call-start = ((), (), s32[]{:S(2)}) async-start(), calls=%async_computation.14 | async-start | bytes 5308416 | tf_op jit(solution)/shard_map/all_gather | solution.py:133
  86.4 15.1 %all-to-all-start = ((bf16[512,4,192]{0,2,1:T(8,128)(2,1)}), bf16[512,4,192]{0,2,1:T(8,128)(2,1)S(1)}, u32[]{:S(2)}, u32[]{:S(2)}) async-start(bf16[512,4,192]{0,2,1:T(8,128)(2,1)} %bitcast.4), calls=%async_computation | async-start | bytes 1572864 | tf_op jit(solution)/shard_map/all_to_all | solution.py:92
  101.5 15.1 %all-to-all-start.2 = ((bf16[512,4,192]{0,2,1:T(8,128)(2,1)}), bf16[512,4,192]{0,2,1:T(8,128)(2,1)S(1)}, u32[]{:S(2)}, u32[]{:S(2)}) async-start(bf16[512,4,192]{0,2,1:T(8,128)(2,1)} %bitcast.8), calls=%async_computation.2 | async-start | bytes 1572864 | tf_op jit(solution)/shard_map/all_to_all | solution.py:94
  116.6 15.1 %all-to-all-start.1 = ((bf16[512,4,192]{0,2,1:T(8,128)(2,1)}), bf16[512,4,192]{0,2,1:T(8,128)(2,1)S(1)}, u32[]{:S(2)}, u32[]{:S(2)}) async-start(bf16[512,4,192]{0,2,1:T(8,128)(2,1)} %bitcast.6), calls=%async_computation.1 | async-start | bytes 1572864 | tf_op jit(solution)/shard_map/all_to_all | solution.py:93
  120.1 161.5 %all-gather.14.cloned.1.call-start = ((), (), s32[]{:S(2)}) async-start(), calls=%async_computation.15 | async-start | bytes 5308416 | tf_op jit(solution)/shard_map/all_gather | solution.py:135
  180.5 29.8 %all-to-all-start.3 = ((bf16[4,512,192]{1,2,0:T(8,128)(2,1)}), bf16[4,512,192]{1,2,0:T(8,128)(2,1)S(1)}, u32[]{:S(2)}, u32[]{:S(2)}) async-start(bf16[4,512,192]{1,2,0:T(8,128)(2,1)} %bitcast.10), calls=%async_computation.3 | async-start | bytes 1572864 | tf_op jit(solution)/shard_map/all_to_all | solution.py:124
  309.4 15.9 %all-to-all-start.4 = ((bf16[512,4,192]{0,2,1:T(8,128)(2,1)}), bf16[512,4,192]{0,2,1:T(8,128)(2,1)}, u32[]{:S(2)}, u32[]{:S(2)}) async-start(bf16[512,4,192]{0,2,1:T(8,128)(2,1)} %bitcast.15), calls=%async_computation.4 | async-start | bytes 1572864 | tf_op jit(solution)/shard_map/all_to_all | solution.py:177
  448.9 15.1 %all-to-all-start.6 = ((bf16[4,512,192]{1,2,0:T(8,128)(2,1)}), bf16[4,512,192]{1,2,0:T(8,128)(2,1)S(1)}, u32[]{:S(2)}, u32[]{:S(2)}) async-start(bf16[4,512,192]{1,2,0:T(8,128)(2,1)} %copy.92), calls=%async_computation.6 | async-start | bytes 1572864 | tf_op jit(solution)/shard_map/all_to_all | solution.py:220
  452.4 173.3 %reduce-scatter.5.cloned.1.call-start = ((), (), s32[]{:S(2)}) async-start(), calls=%async_computation.16 | async-start | bytes 7962624 | tf_op jit(solution)/shard_map/reduce_scatter | solution.py:256
  499.3 198.2 %reduce-scatter.7.cloned.1.call-start = ((), (), s32[]{:S(2)}) async-start(), calls=%async_computation.17 | async-start | bytes 2654208 | tf_op jit(solution)/shard_map/reduce_scatter | solution.py:258
  502.9 361.2 %reduce-scatter.11.cloned.1.call-start = ((), (), s32[]{:S(2)}) async-start(), calls=%async_computation.19 | async-start | bytes 10616832 | tf_op jit(solution)/shard_map/reduce_scatter | solution.py:264
  511.8 518.9 %reduce-scatter.9.cloned.1.call-start = ((), (), s32[]{:S(2)}) async-start(), calls=%async_computation.18 | async-start | bytes 10616832 | tf_op jit(solution)/shard_map/reduce_scatter | solution.py:262
  520.4 566.9 %all-gather.16.cloned.1.call-start = ((), (), s32[]{:S(2)}) async-start(), calls=%async_computation.20 | async-start | bytes 2211840 | tf_op jit(solution)/shard_map/all_gather | solution.py:269
  627.8 468.5 %all-reduce.21.cloned.1.call-start = ((), (), s32[]{:S(2)}) async-start(), calls=%async_computation.21 | async-start | bytes 2654208 | tf_op jit(solution)/shard_map/psum | solution.py:288
  635.8 397.7 %copy-start.32 = (f32[768]{0:T(1024)S(1)}, f32[768]{0:T(1024)}, u32[]{:S(2)}) copy-start(f32[768]{0:T(1024)} %get-tuple-element.296) | copy-start | bytes 9220
  635.8 397.7 %copy-start.33 = (f32[768]{0:T(1024)S(1)}, f32[768]{0:T(1024)}, u32[]{:S(2)}) copy-start(f32[768]{0:T(1024)} %get-tuple-element.299) | copy-start | bytes 9220
  635.8 397.7 %copy-start.34 = (f32[768]{0:T(1024)S(1)}, f32[768]{0:T(1024)}, u32[]{:S(2)}) copy-start(f32[768]{0:T(1024)} %get-tuple-element.370) | copy-start | bytes 9220
  635.9 397.7 %copy-start.35 = (f32[768]{0:T(1024)S(1)}, f32[768]{0:T(1024)}, u32[]{:S(2)}) copy-start(f32[768]{0:T(1024)} %get-tuple-element.374) | copy-start | bytes 9220
  635.9 397.7 %copy-start.38 = (f32[3072]{0:T(1024)S(1)}, f32[3072]{0:T(1024)}, u32[]{:S(2)}) copy-start(f32[3072]{0:T(1024)} %get-tuple-element.372) | copy-start | bytes 36868
  635.9 397.7 %copy-start.47 = (f32[768]{0:T(1024)S(1)}, f32[768]{0:T(1024)}, u32[]{:S(2)}) copy-start(f32[768]{0:T(1024)} %get-tuple-element.294) | copy-start | bytes 9220
  635.9 397.7 %copy-start.48 = (f32[768]{0:T(1024)S(1)}, f32[768]{0:T(1024)}, u32[]{:S(2)}) copy-start(f32[768]{0:T(1024)} %get-tuple-element.298) | copy-start | bytes 9220
  635.9 433.9 %copy-start.29 = (s32[512]{0:T(512)S(1)}, s32[512]{0:T(512)}, u32[]{:S(2)}) copy-start(s32[512]{0:T(512)} %copy-done.28) | copy-start | bytes 6148
  (55 other events, 2303.3 us)
Sparse Core Ops, SparseCore 0:
  10.2 68.4 all-gather.7
  80.9 39.5 all-gather.9
  122.7 78.6 all-gather.11
  203.4 78.1 all-gather.13
  499.5 126.2 reduce-scatter.4
  629.5 68.0 reduce-scatter.6
  701.6 162.5 reduce-scatter.10
  868.2 162.5 reduce-scatter.8
  1032.4 19.8 all-gather.15
  1056.0 40.1 all-reduce.20
